TPU v7x, 512 devices: a whole 4x4x16 slice. The times are simulated.
512 devices in a mesh: dp: 8 (over y, core), ctx: 64 (over z, x).
Axes of the slice: x: 4, y: 4, z: 16, core: 2. Of those that a mesh axis runs over, the one named last changes fastest.
Arguments:
- query_in: bfloat16 [8, 8192, 1792], P('dp', 'ctx'), may hold values from -8 to 8
- key_in: bfloat16 [8, 8192, 256], P('dp', 'ctx'), may hold values from -4 to 4
- value_input: bfloat16 [8, 8192, 256], P('dp', 'ctx'), may hold values from -4 to 4
- output_gradient: bfloat16 [8, 8192, 1792], P('dp', 'ctx'), may hold values from -5 to 5
- doc_ids: int32 [8, 8192], P('dp', 'ctx'), may hold values from 0 to 1, as said below
- query_bias: float32 [1792], replicated, may hold values from -2 to 2
Outputs:
- attended: bfloat16 [8, 8192, 1792], P('dp', 'ctx')
- grad_query: bfloat16 [8, 8192, 1792], P('dp', 'ctx')
- key_gradient: bfloat16 [8, 8192, 256], P('dp', 'ctx')
- value_gradient: bfloat16 [8, 8192, 256], P('dp', 'ctx')
- grad_bias: float32 [1792], replicated
Inputs may be any that keep to these rules, and one draw needn't show every extreme that they name: `doc_ids`: ids never fall along a sequence; each of the 2 documents of a sequence holds 2048 to 6144 tokens, and together they fill all 8192 tokens.
All inputs are finite; a program needn't handle non-finite values.
Results may differ from a plain program's by a relative error of at most 0.019.
Values may be sent and summed in bfloat16 or wider, within the bound.
A program may use at most 64 MiB of HBM per device.

v0:
```python
import math
import jax
import jax.numpy as jnp
from jax import lax
from jax.sharding import PartitionSpec as P

QUERY_HEADS = 14
KEY_VALUE_HEADS = 2
HEAD_SIZE = 128
GROUP_SIZE = 7
BLK = 128
WB = 16


def passed_along(value, axis, steps):
    count = lax.axis_size(axis)
    first, last = (max(0, -steps), min(count, count - steps))
    return lax.ppermute(value, axis, [(source, source + steps) for source in range(first, last)])


def split_pack(packed_block):
    head_size_width = KEY_VALUE_HEADS * HEAD_SIZE
    key_head_rows = packed_block[:, :head_size_width].reshape(
        packed_block.shape[0], KEY_VALUE_HEADS, HEAD_SIZE
    )
    value_head_rows = packed_block[:, head_size_width:].reshape(
        packed_block.shape[0], KEY_VALUE_HEADS, HEAD_SIZE
    )
    return (key_head_rows, value_head_rows)


def local(query_in, key_in, value_input, output_gradient, doc_ids, query_bias):
    sharded_rows = query_in.shape[1]
    ctx_count = lax.axis_size("ctx")
    ctx_rank = lax.axis_index("ctx")
    score_scale = 1.0 / math.sqrt(HEAD_SIZE)
    blocks_here = sharded_rows // BLK
    window_slots = min((WB - 1 + blocks_here - 1) // blocks_here, ctx_count - 1) + 1
    group_slots = max(1, min(window_slots, 512 // sharded_rows))
    group_count = -(-window_slots // group_slots)
    padded_slots = group_count * group_slots
    grouped_rows = group_slots * sharded_rows
    packed_width = 2 * KEY_VALUE_HEADS * HEAD_SIZE
    query_rows = (query_in[0].astype(jnp.float32) + query_bias).astype(jnp.bfloat16)
    query_head_rows = query_rows.reshape(sharded_rows, KEY_VALUE_HEADS, GROUP_SIZE, HEAD_SIZE)
    gradient_heads = output_gradient[0].reshape(
        sharded_rows, KEY_VALUE_HEADS, GROUP_SIZE, HEAD_SIZE
    )
    own_pack = jnp.concatenate([key_in[0], value_input[0]], axis=1)
    own_docs = doc_ids[0]
    query_pos = ctx_rank * sharded_rows + jnp.arange(sharded_rows, dtype=jnp.int32)
    first_pack = jnp.concatenate(
        [own_pack[None], jnp.zeros((window_slots - 1, sharded_rows, packed_width), jnp.bfloat16)],
        axis=0,
    )
    first_docs = jnp.concatenate(
        [own_docs[None], jnp.zeros((window_slots - 1, sharded_rows), jnp.int32)], axis=0
    )

    def pass_on(step_index, running):
        stored_pack, stored_docs, moving_pack, moving_docs = running
        moving_pack, moving_docs = passed_along((moving_pack, moving_docs), "ctx", 1)
        stored_pack = lax.dynamic_update_index_in_dim(stored_pack, moving_pack, step_index, 0)
        stored_docs = lax.dynamic_update_index_in_dim(stored_docs, moving_docs, step_index, 0)
        return (stored_pack, stored_docs, moving_pack, moving_docs)

    window_pack, window_docs, _, _ = lax.fori_loop(
        1, window_slots, pass_on, (first_pack, first_docs, own_pack, own_docs)
    )
    spare_slots = padded_slots - window_slots
    window_pack = jnp.concatenate(
        [window_pack, jnp.zeros((spare_slots, sharded_rows, packed_width), jnp.bfloat16)], axis=0
    )
    window_pack = window_pack.reshape(group_count, grouped_rows, packed_width)
    window_docs = jnp.concatenate(
        [window_docs, jnp.zeros((spare_slots, sharded_rows), jnp.int32)], axis=0
    )
    window_docs = window_docs.reshape(group_count, grouped_rows)
    group_ids = jnp.arange(group_count, dtype=jnp.int32)

    def group_mask(group_index, docs_block):
        key_index = jnp.arange(grouped_rows, dtype=jnp.int32)
        slot_index = group_index * group_slots + key_index // sharded_rows
        key_pos = (ctx_rank - slot_index) * sharded_rows + key_index % sharded_rows
        inside = ((slot_index < window_slots) & (key_pos >= 0))[None, :]
        causal = key_pos[None, :] <= query_pos[:, None]
        near = query_pos[:, None] // BLK - key_pos[None, :] // BLK < WB
        same_doc = own_docs[:, None] == docs_block[None, :]
        return inside & causal & near & same_doc

    def group_scores(packed_block, allowed):
        key_head_rows, value_head_rows = split_pack(packed_block)
        scores = (
            jnp.einsum(
                "qgnd,kgd->gnqk", query_head_rows, key_head_rows, preferred_element_type=jnp.float32
            )
            * score_scale
        )
        return (jnp.where(allowed[None, None], scores, -jnp.inf), key_head_rows, value_head_rows)

    def forward_work(running, packed_block, allowed):
        row_max, row_sum, weighted = running
        scores, key_head_rows, value_head_rows = group_scores(packed_block, allowed)
        new_max = jnp.maximum(row_max, jnp.max(scores, axis=-1))
        rescale = jnp.exp(row_max - new_max)
        weights = jnp.exp(scores - new_max[..., None])
        row_sum = row_sum * rescale + jnp.sum(weights, axis=-1)
        weighted = weighted * rescale[..., None] + jnp.einsum(
            "gnqk,kgd->gnqd", weights, value_head_rows.astype(jnp.float32)
        )
        return (new_max, row_sum, weighted)

    def forward_step(running, inputs):
        packed_block, docs_block, group_index = inputs
        allowed = group_mask(group_index, docs_block)
        running = forward_work(running, packed_block, allowed)
        return (running, None)

    statistics_shape = (KEY_VALUE_HEADS, GROUP_SIZE, sharded_rows)
    start_stats = (
        jnp.full(statistics_shape, -jnp.inf, jnp.float32),
        jnp.zeros(statistics_shape, jnp.float32),
        jnp.zeros(statistics_shape + (HEAD_SIZE,), jnp.float32),
    )
    (row_max, row_sum, weighted), _ = lax.scan(
        forward_step, start_stats, (window_pack, window_docs, group_ids)
    )
    log_total = row_max + jnp.log(row_sum)
    attended = jnp.transpose(weighted / row_sum[..., None], (2, 0, 1, 3)).astype(jnp.bfloat16)
    row_dot = jnp.einsum(
        "qgnd,qgnd->gnq", gradient_heads, attended, preferred_element_type=jnp.float32
    )

    def backward_work(grad_query, packed_block, allowed):
        scores, key_head_rows, value_head_rows = group_scores(packed_block, allowed)
        attend = jnp.exp(scores - log_total[..., None])
        grad_prob = jnp.einsum(
            "qgnd,kgd->gnqk", gradient_heads, value_head_rows, preferred_element_type=jnp.float32
        )
        grad_score = (attend * (grad_prob - row_dot[..., None])).astype(jnp.bfloat16)
        grad_query = grad_query + jnp.einsum(
            "gnqk,kgd->qgnd", grad_score, key_head_rows, preferred_element_type=jnp.float32
        )
        key_gradient = (
            jnp.einsum(
                "gnqk,qgnd->kgd", grad_score, query_head_rows, preferred_element_type=jnp.float32
            )
            * score_scale
        )
        value_gradient = jnp.einsum(
            "gnqk,qgnd->kgd",
            attend.astype(jnp.bfloat16),
            gradient_heads,
            preferred_element_type=jnp.float32,
        )
        partial_value = jnp.concatenate(
            [
                key_gradient.reshape(grouped_rows, KEY_VALUE_HEADS * HEAD_SIZE),
                value_gradient.reshape(grouped_rows, KEY_VALUE_HEADS * HEAD_SIZE),
            ],
            axis=1,
        )
        return (grad_query, partial_value)

    def backward_step(grad_query, inputs):
        packed_block, docs_block, group_index = inputs
        allowed = group_mask(group_index, docs_block)
        return backward_work(grad_query, packed_block, allowed)

    grad_query, partials = lax.scan(
        backward_step,
        jnp.zeros((sharded_rows, KEY_VALUE_HEADS, GROUP_SIZE, HEAD_SIZE), jnp.float32),
        (window_pack, window_docs, group_ids),
    )
    partials = partials.reshape(padded_slots, sharded_rows, packed_width)
    query_grad = (grad_query * score_scale).reshape(sharded_rows, QUERY_HEADS * HEAD_SIZE)

    def return_partial(step_index, running):
        returned = passed_along(running, "ctx", -1)
        return returned + lax.dynamic_index_in_dim(
            partials, window_slots - 1 - step_index, 0, keepdims=False
        )

    summed_total = lax.fori_loop(1, window_slots, return_partial, partials[window_slots - 1])
    key_gradient = summed_total[:, : KEY_VALUE_HEADS * HEAD_SIZE].astype(jnp.bfloat16)
    value_gradient = summed_total[:, KEY_VALUE_HEADS * HEAD_SIZE :].astype(jnp.bfloat16)
    grad_bias = lax.psum(jnp.sum(query_grad, axis=0), ("dp", "ctx"))
    attended_out = attended.reshape(sharded_rows, QUERY_HEADS * HEAD_SIZE)
    return (
        attended_out[None],
        query_grad.astype(jnp.bfloat16)[None],
        key_gradient[None],
        value_gradient[None],
        grad_bias,
    )


def solution(mesh):
    placed = (
        P("dp", "ctx", None),
        P("dp", "ctx", None),
        P("dp", "ctx", None),
        P("dp", "ctx", None),
        P("dp", "ctx"),
        P(),
    )
    return jax.shard_map(
        local,
        mesh=mesh,
        in_specs=placed,
        out_specs=(
            P("dp", "ctx", None),
            P("dp", "ctx", None),
            P("dp", "ctx", None),
            P("dp", "ctx", None),
            P(),
        ),
        check_vma=False,
    )
```

profile of v0, /device:TPU:1, one launch (start us, length us, event | category | flops | bytes accessed | tf_op | source)
XLA Modules:
  0.0 563.7 jit_solution(16847469983181574787)
XLA Ops:
  8.9 138.4 %while.72 = (s32[]{:T(128)}, bf16[16,128,512]{2,1,0:T(8,128)(2,1)}, s32[16,128]{1,0:T(8,128)S(1)}, bf16[128,512]{1,0:T(8,128)(2,1)S(1)}, s32[128]{0:T(128)S(1)}, /*index=5*/s32[]{:T(128)}, s32[]{:T(128)}, s32[]{:T(128)}) while((s32[]{:T(128)}, bf16[16,128,512]{2,1,0:T(8,128)(2,1)}, s32[16,128]{1,0:T(8,128)S(1)}, ...), condition=%wide.region_1.2_spmd, body=%wide.region_0.1_spmd.sunk | while | flops 5 | bytes 1052879 | solution.py:67
  29.2 4.8 collective-permute-start.1
  102.5 4.8 collective-permute-start.1
  131.0 4.5 collective-permute-start.1
  140.5 5.3 collective-permute-start.1
  151.5 23.1 %while.74 = (s32[]{:T(128)}, f32[2,7,128]{2,1,0:T(8,128)S(1)}, f32[2,7,128]{2,1,0:T(8,128)S(1)}, f32[2,7,128,128]{3,2,1,0:T(8,128)S(1)}, s32[4]{0:T(128)S(1)}, /...) while((s32[]{:T(128)}, f32[2,7,128]{2,1,0:T(8,128)S(1)}, ...), condition=%wide.region_5.6_spmd.clone.clone.clone, body=%wide.region_2.5_spmd.clone.clone.clone.sunk | while | flops 480120704 | bytes 16320205 | solution.py:125
  179.3 42.8 %while.75 = (s32[]{:T(128)}, f32[128,2,7,128]{0,3,2,1:T(8,128)S(1)}, f32[4,512,512]{2,1,0:T(8,128)}, bf16[4,512,512]{1,2,0:T(8,128)(2,1)}, s32[4]{0:T(128)S(1)},...) while((s32[]{:T(128)}, ...), condition=%wide.region_7.8_spmd.clone.clone.clone, body=%wide.region_6.7_spmd.clone.clone.clone.sunk | while | flops 1184918656 | bytes 30644960 | solution.py:170
  223.1 163.2 %while.73 = (s32[]{:T(128)}, f32[128,512]{1,0:T(8,128)S(1)}, f32[16,128,512]{2,1,0:T(8,128)}, s32[]{:T(128)}, s32[]{:T(128)}, /*index=5*/s32[]{:T(128)}, s32[]{:T(128)}) while((s32[]{:T(128)}, f32[128,512]{1,0:T(8,128)S(1)}, f32[16,128,512]{2,1,0:T(8,128)}, s32[]{:T(128)}, s32[]{:T(128)}, /*index=5*/s32[]{:T(128)}, s32[]{:T(128)}) %tuple.177), condition=%wide.region_9.10_spmd, body=%wide.region_8.9_spmd.sunk | while | flops 65542 | bytes 1835175 | solution.py:184
  224.4 6.0 %collective-permute-done.2 = f32[128,512]{1,0:T(8,128)S(1)} collective-permute-done((f32[128,512]{1,0:T(8,128)S(1)}, f32[128,512]{1,0:T(8,128)S(1)}, u32[]{:S(2)}, u32[]{:S(2)}) %collective-permute-start.2) | collective-permute-done | bytes 262176 | tf_op jit(solution)/shard_map/while/body/eval_jaxpr/ppermute | solution.py:18
  232.7 7.8 %collective-permute-done.2 = f32[128,512]{1,0:T(8,128)S(1)} collective-permute-done((f32[128,512]{1,0:T(8,128)S(1)}, f32[128,512]{1,0:T(8,128)S(1)}, u32[]{:S(2)}, u32[]{:S(2)}) %collective-permute-start.2) | collective-permute-done | bytes 262176 | tf_op jit(solution)/shard_map/while/body/eval_jaxpr/ppermute | solution.py:18
  242.8 7.7 %collective-permute-done.2 = f32[128,512]{1,0:T(8,128)S(1)} collective-permute-done((f32[128,512]{1,0:T(8,128)S(1)}, f32[128,512]{1,0:T(8,128)S(1)}, u32[]{:S(2)}, u32[]{:S(2)}) %collective-permute-start.2) | collective-permute-done | bytes 262176 | tf_op jit(solution)/shard_map/while/body/eval_jaxpr/ppermute | solution.py:18
  252.8 10.2 %collective-permute-done.2 = f32[128,512]{1,0:T(8,128)S(1)} collective-permute-done((f32[128,512]{1,0:T(8,128)S(1)}, f32[128,512]{1,0:T(8,128)S(1)}, u32[]{:S(2)}, u32[]{:S(2)}) %collective-permute-start.2) | collective-permute-done | bytes 262176 | tf_op jit(solution)/shard_map/while/body/eval_jaxpr/ppermute | solution.py:18
  265.3 11.4 %collective-permute-done.2 = f32[128,512]{1,0:T(8,128)S(1)} collective-permute-done((f32[128,512]{1,0:T(8,128)S(1)}, f32[128,512]{1,0:T(8,128)S(1)}, u32[]{:S(2)}, u32[]{:S(2)}) %collective-permute-start.2) | collective-permute-done | bytes 262176 | tf_op jit(solution)/shard_map/while/body/eval_jaxpr/ppermute | solution.py:18
  279.0 9.2 %collective-permute-done.2 = f32[128,512]{1,0:T(8,128)S(1)} collective-permute-done((f32[128,512]{1,0:T(8,128)S(1)}, f32[128,512]{1,0:T(8,128)S(1)}, u32[]{:S(2)}, u32[]{:S(2)}) %collective-permute-start.2) | collective-permute-done | bytes 262176 | tf_op jit(solution)/shard_map/while/body/eval_jaxpr/ppermute | solution.py:18
  290.5 7.4 %collective-permute-done.2 = f32[128,512]{1,0:T(8,128)S(1)} collective-permute-done((f32[128,512]{1,0:T(8,128)S(1)}, f32[128,512]{1,0:T(8,128)S(1)}, u32[]{:S(2)}, u32[]{:S(2)}) %collective-permute-start.2) | collective-permute-done | bytes 262176 | tf_op jit(solution)/shard_map/while/body/eval_jaxpr/ppermute | solution.py:18
  300.1 6.8 %collective-permute-done.2 = f32[128,512]{1,0:T(8,128)S(1)} collective-permute-done((f32[128,512]{1,0:T(8,128)S(1)}, f32[128,512]{1,0:T(8,128)S(1)}, u32[]{:S(2)}, u32[]{:S(2)}) %collective-permute-start.2) | collective-permute-done | bytes 262176 | tf_op jit(solution)/shard_map/while/body/eval_jaxpr/ppermute | solution.py:18
  309.3 7.6 %collective-permute-done.2 = f32[128,512]{1,0:T(8,128)S(1)} collective-permute-done((f32[128,512]{1,0:T(8,128)S(1)}, f32[128,512]{1,0:T(8,128)S(1)}, u32[]{:S(2)}, u32[]{:S(2)}) %collective-permute-start.2) | collective-permute-done | bytes 262176 | tf_op jit(solution)/shard_map/while/body/eval_jaxpr/ppermute | solution.py:18
  319.2 7.9 %collective-permute-done.2 = f32[128,512]{1,0:T(8,128)S(1)} collective-permute-done((f32[128,512]{1,0:T(8,128)S(1)}, f32[128,512]{1,0:T(8,128)S(1)}, u32[]{:S(2)}, u32[]{:S(2)}) %collective-permute-start.2) | collective-permute-done | bytes 262176 | tf_op jit(solution)/shard_map/while/body/eval_jaxpr/ppermute | solution.py:18
  329.4 7.9 %collective-permute-done.2 = f32[128,512]{1,0:T(8,128)S(1)} collective-permute-done((f32[128,512]{1,0:T(8,128)S(1)}, f32[128,512]{1,0:T(8,128)S(1)}, u32[]{:S(2)}, u32[]{:S(2)}) %collective-permute-start.2) | collective-permute-done | bytes 262176 | tf_op jit(solution)/shard_map/while/body/eval_jaxpr/ppermute | solution.py:18
  339.7 7.9 %collective-permute-done.2 = f32[128,512]{1,0:T(8,128)S(1)} collective-permute-done((f32[128,512]{1,0:T(8,128)S(1)}, f32[128,512]{1,0:T(8,128)S(1)}, u32[]{:S(2)}, u32[]{:S(2)}) %collective-permute-start.2) | collective-permute-done | bytes 262176 | tf_op jit(solution)/shard_map/while/body/eval_jaxpr/ppermute | solution.py:18
  349.9 8.8 %collective-permute-done.2 = f32[128,512]{1,0:T(8,128)S(1)} collective-permute-done((f32[128,512]{1,0:T(8,128)S(1)}, f32[128,512]{1,0:T(8,128)S(1)}, u32[]{:S(2)}, u32[]{:S(2)}) %collective-permute-start.2) | collective-permute-done | bytes 262176 | tf_op jit(solution)/shard_map/while/body/eval_jaxpr/ppermute | solution.py:18
  361.0 10.4 %collective-permute-done.2 = f32[128,512]{1,0:T(8,128)S(1)} collective-permute-done((f32[128,512]{1,0:T(8,128)S(1)}, f32[128,512]{1,0:T(8,128)S(1)}, u32[]{:S(2)}, u32[]{:S(2)}) %collective-permute-start.2) | collective-permute-done | bytes 262176 | tf_op jit(solution)/shard_map/while/body/eval_jaxpr/ppermute | solution.py:18
  373.7 11.5 %collective-permute-done.2 = f32[128,512]{1,0:T(8,128)S(1)} collective-permute-done((f32[128,512]{1,0:T(8,128)S(1)}, f32[128,512]{1,0:T(8,128)S(1)}, u32[]{:S(2)}, u32[]{:S(2)}) %collective-permute-start.2) | collective-permute-done | bytes 262176 | tf_op jit(solution)/shard_map/while/body/eval_jaxpr/ppermute | solution.py:18
  387.3 175.4 %psum.7 = f32[1792]{0:T(1024)} all-reduce(f32[1792]{0:T(1024)S(1)} %reduce_sum.25), channel_id=1, replica_groups=mesh['dp'=8,'ctx'=64] {'dp','ctx'}, use_global_device_ids=true, to_apply=%region_11.12 | all-reduce | flops 1792 | bytes 14336 | tf_op jit(solution)/shard_map/psum | solution.py:187
  (298 shorter events, 232.6 us)
Async XLA Ops:
  25.7 9.1 %collective-permute-start = (bf16[128,512]{1,0:T(8,128)(2,1)S(1)}, bf16[128,512]{1,0:T(8,128)(2,1)S(1)}, u32[]{:S(2)}, u32[]{:S(2)}) collective-permute-start(bf16[128,512]{1,0:T(8,128)(2,1)S(1)} %get-tuple-element.1222), channel_id=1, source_target_pairs={{0,1},{1,2},{2,3},{3,4},{4,5},{5,6},{6,7},{7,8},{8,9},{9,10},{10,1... | collective-permute-start | bytes 393224 | tf_op jit(solution)/shard_map/while/body/eval_jaxpr/ppermute | solution.py:18
  35.5 8.3 %collective-permute-start = (bf16[128,512]{1,0:T(8,128)(2,1)S(1)}, bf16[128,512]{1,0:T(8,128)(2,1)S(1)}, u32[]{:S(2)}, u32[]{:S(2)}) collective-permute-start(bf16[128,512]{1,0:T(8,128)(2,1)S(1)} %get-tuple-element.1222), channel_id=1, source_target_pairs={{0,1},{1,2},{2,3},{3,4},{4,5},{5,6},{6,7},{7,8},{8,9},{9,10},{10,1... | collective-permute-start | bytes 393224 | tf_op jit(solution)/shard_map/while/body/eval_jaxpr/ppermute | solution.py:18
  44.5 8.3 %collective-permute-start = (bf16[128,512]{1,0:T(8,128)(2,1)S(1)}, bf16[128,512]{1,0:T(8,128)(2,1)S(1)}, u32[]{:S(2)}, u32[]{:S(2)}) collective-permute-start(bf16[128,512]{1,0:T(8,128)(2,1)S(1)} %get-tuple-element.1222), channel_id=1, source_target_pairs={{0,1},{1,2},{2,3},{3,4},{4,5},{5,6},{6,7},{7,8},{8,9},{9,10},{10,1... | collective-permute-start | bytes 393224 | tf_op jit(solution)/shard_map/while/body/eval_jaxpr/ppermute | solution.py:18
  53.5 8.3 %collective-permute-start = (bf16[128,512]{1,0:T(8,128)(2,1)S(1)}, bf16[128,512]{1,0:T(8,128)(2,1)S(1)}, u32[]{:S(2)}, u32[]{:S(2)}) collective-permute-start(bf16[128,512]{1,0:T(8,128)(2,1)S(1)} %get-tuple-element.1222), channel_id=1, source_target_pairs={{0,1},{1,2},{2,3},{3,4},{4,5},{5,6},{6,7},{7,8},{8,9},{9,10},{10,1... | collective-permute-start | bytes 393224 | tf_op jit(solution)/shard_map/while/body/eval_jaxpr/ppermute | solution.py:18
  62.6 8.3 %collective-permute-start = (bf16[128,512]{1,0:T(8,128)(2,1)S(1)}, bf16[128,512]{1,0:T(8,128)(2,1)S(1)}, u32[]{:S(2)}, u32[]{:S(2)}) collective-permute-start(bf16[128,512]{1,0:T(8,128)(2,1)S(1)} %get-tuple-element.1222), channel_id=1, source_target_pairs={{0,1},{1,2},{2,3},{3,4},{4,5},{5,6},{6,7},{7,8},{8,9},{9,10},{10,1... | collective-permute-start | bytes 393224 | tf_op jit(solution)/shard_map/while/body/eval_jaxpr/ppermute | solution.py:18
  80.6 8.4 %collective-permute-start = (bf16[128,512]{1,0:T(8,128)(2,1)S(1)}, bf16[128,512]{1,0:T(8,128)(2,1)S(1)}, u32[]{:S(2)}, u32[]{:S(2)}) collective-permute-start(bf16[128,512]{1,0:T(8,128)(2,1)S(1)} %get-tuple-element.1222), channel_id=1, source_target_pairs={{0,1},{1,2},{2,3},{3,4},{4,5},{5,6},{6,7},{7,8},{8,9},{9,10},{10,1... | collective-permute-start | bytes 393224 | tf_op jit(solution)/shard_map/while/body/eval_jaxpr/ppermute | solution.py:18
  89.7 8.6 %collective-permute-start = (bf16[128,512]{1,0:T(8,128)(2,1)S(1)}, bf16[128,512]{1,0:T(8,128)(2,1)S(1)}, u32[]{:S(2)}, u32[]{:S(2)}) collective-permute-start(bf16[128,512]{1,0:T(8,128)(2,1)S(1)} %get-tuple-element.1222), channel_id=1, source_target_pairs={{0,1},{1,2},{2,3},{3,4},{4,5},{5,6},{6,7},{7,8},{8,9},{9,10},{10,1... | collective-permute-start | bytes 393224 | tf_op jit(solution)/shard_map/while/body/eval_jaxpr/ppermute | solution.py:18
  99.0 9.1 %collective-permute-start = (bf16[128,512]{1,0:T(8,128)(2,1)S(1)}, bf16[128,512]{1,0:T(8,128)(2,1)S(1)}, u32[]{:S(2)}, u32[]{:S(2)}) collective-permute-start(bf16[128,512]{1,0:T(8,128)(2,1)S(1)} %get-tuple-element.1222), channel_id=1, source_target_pairs={{0,1},{1,2},{2,3},{3,4},{4,5},{5,6},{6,7},{7,8},{8,9},{9,10},{10,1... | collective-permute-start | bytes 393224 | tf_op jit(solution)/shard_map/while/body/eval_jaxpr/ppermute | solution.py:18
  108.8 8.6 %collective-permute-start = (bf16[128,512]{1,0:T(8,128)(2,1)S(1)}, bf16[128,512]{1,0:T(8,128)(2,1)S(1)}, u32[]{:S(2)}, u32[]{:S(2)}) collective-permute-start(bf16[128,512]{1,0:T(8,128)(2,1)S(1)} %get-tuple-element.1222), channel_id=1, source_target_pairs={{0,1},{1,2},{2,3},{3,4},{4,5},{5,6},{6,7},{7,8},{8,9},{9,10},{10,1... | collective-permute-start | bytes 393224 | tf_op jit(solution)/shard_map/while/body/eval_jaxpr/ppermute | solution.py:18
  127.1 9.1 %collective-permute-start = (bf16[128,512]{1,0:T(8,128)(2,1)S(1)}, bf16[128,512]{1,0:T(8,128)(2,1)S(1)}, u32[]{:S(2)}, u32[]{:S(2)}) collective-permute-start(bf16[128,512]{1,0:T(8,128)(2,1)S(1)} %get-tuple-element.1222), channel_id=1, source_target_pairs={{0,1},{1,2},{2,3},{3,4},{4,5},{5,6},{6,7},{7,8},{8,9},{9,10},{10,1... | collective-permute-start | bytes 393224 | tf_op jit(solution)/shard_map/while/body/eval_jaxpr/ppermute | solution.py:18
  137.0 9.7 %collective-permute-start = (bf16[128,512]{1,0:T(8,128)(2,1)S(1)}, bf16[128,512]{1,0:T(8,128)(2,1)S(1)}, u32[]{:S(2)}, u32[]{:S(2)}) collective-permute-start(bf16[128,512]{1,0:T(8,128)(2,1)S(1)} %get-tuple-element.1222), channel_id=1, source_target_pairs={{0,1},{1,2},{2,3},{3,4},{4,5},{5,6},{6,7},{7,8},{8,9},{9,10},{10,1... | collective-permute-start | bytes 393224 | tf_op jit(solution)/shard_map/while/body/eval_jaxpr/ppermute | solution.py:18
  231.4 9.1 %collective-permute-start.2 = (f32[128,512]{1,0:T(8,128)S(1)}, f32[128,512]{1,0:T(8,128)S(1)}, u32[]{:S(2)}, u32[]{:S(2)}) collective-permute-start(f32[128,512]{1,0:T(8,128)S(1)} %get-tuple-element.1333), channel_id=1, source_target_pairs={{1,0},{2,1},{3,2},{4,3},{5,4},{6,5},{7,6},{8,7},{9,8},{10,9},{11,1... | collective-permute-start | bytes 786440 | tf_op jit(solution)/shard_map/while/body/eval_jaxpr/ppermute | solution.py:18
  241.5 9.0 %collective-permute-start.2 = (f32[128,512]{1,0:T(8,128)S(1)}, f32[128,512]{1,0:T(8,128)S(1)}, u32[]{:S(2)}, u32[]{:S(2)}) collective-permute-start(f32[128,512]{1,0:T(8,128)S(1)} %get-tuple-element.1333), channel_id=1, source_target_pairs={{1,0},{2,1},{3,2},{4,3},{5,4},{6,5},{7,6},{8,7},{9,8},{10,9},{11,1... | collective-permute-start | bytes 786440 | tf_op jit(solution)/shard_map/while/body/eval_jaxpr/ppermute | solution.py:18
  251.5 11.5 %collective-permute-start.2 = (f32[128,512]{1,0:T(8,128)S(1)}, f32[128,512]{1,0:T(8,128)S(1)}, u32[]{:S(2)}, u32[]{:S(2)}) collective-permute-start(f32[128,512]{1,0:T(8,128)S(1)} %get-tuple-element.1333), channel_id=1, source_target_pairs={{1,0},{2,1},{3,2},{4,3},{5,4},{6,5},{7,6},{8,7},{9,8},{10,9},{11,1... | collective-permute-start | bytes 786440 | tf_op jit(solution)/shard_map/while/body/eval_jaxpr/ppermute | solution.py:18
  264.0 12.7 %collective-permute-start.2 = (f32[128,512]{1,0:T(8,128)S(1)}, f32[128,512]{1,0:T(8,128)S(1)}, u32[]{:S(2)}, u32[]{:S(2)}) collective-permute-start(f32[128,512]{1,0:T(8,128)S(1)} %get-tuple-element.1333), channel_id=1, source_target_pairs={{1,0},{2,1},{3,2},{4,3},{5,4},{6,5},{7,6},{8,7},{9,8},{10,9},{11,1... | collective-permute-start | bytes 786440 | tf_op jit(solution)/shard_map/while/body/eval_jaxpr/ppermute | solution.py:18
  277.7 10.5 %collective-permute-start.2 = (f32[128,512]{1,0:T(8,128)S(1)}, f32[128,512]{1,0:T(8,128)S(1)}, u32[]{:S(2)}, u32[]{:S(2)}) collective-permute-start(f32[128,512]{1,0:T(8,128)S(1)} %get-tuple-element.1333), channel_id=1, source_target_pairs={{1,0},{2,1},{3,2},{4,3},{5,4},{6,5},{7,6},{8,7},{9,8},{10,9},{11,1... | collective-permute-start | bytes 786440 | tf_op jit(solution)/shard_map/while/body/eval_jaxpr/ppermute | solution.py:18
  289.2 8.7 %collective-permute-start.2 = (f32[128,512]{1,0:T(8,128)S(1)}, f32[128,512]{1,0:T(8,128)S(1)}, u32[]{:S(2)}, u32[]{:S(2)}) collective-permute-start(f32[128,512]{1,0:T(8,128)S(1)} %get-tuple-element.1333), channel_id=1, source_target_pairs={{1,0},{2,1},{3,2},{4,3},{5,4},{6,5},{7,6},{8,7},{9,8},{10,9},{11,1... | collective-permute-start | bytes 786440 | tf_op jit(solution)/shard_map/while/body/eval_jaxpr/ppermute | solution.py:18
  308.0 8.9 %collective-permute-start.2 = (f32[128,512]{1,0:T(8,128)S(1)}, f32[128,512]{1,0:T(8,128)S(1)}, u32[]{:S(2)}, u32[]{:S(2)}) collective-permute-start(f32[128,512]{1,0:T(8,128)S(1)} %get-tuple-element.1333), channel_id=1, source_target_pairs={{1,0},{2,1},{3,2},{4,3},{5,4},{6,5},{7,6},{8,7},{9,8},{10,9},{11,1... | collective-permute-start | bytes 786440 | tf_op jit(solution)/shard_map/while/body/eval_jaxpr/ppermute | solution.py:18
  317.9 9.2 %collective-permute-start.2 = (f32[128,512]{1,0:T(8,128)S(1)}, f32[128,512]{1,0:T(8,128)S(1)}, u32[]{:S(2)}, u32[]{:S(2)}) collective-permute-start(f32[128,512]{1,0:T(8,128)S(1)} %get-tuple-element.1333), channel_id=1, source_target_pairs={{1,0},{2,1},{3,2},{4,3},{5,4},{6,5},{7,6},{8,7},{9,8},{10,9},{11,1... | collective-permute-start | bytes 786440 | tf_op jit(solution)/shard_map/while/body/eval_jaxpr/ppermute | solution.py:18
  328.1 9.2 %collective-permute-start.2 = (f32[128,512]{1,0:T(8,128)S(1)}, f32[128,512]{1,0:T(8,128)S(1)}, u32[]{:S(2)}, u32[]{:S(2)}) collective-permute-start(f32[128,512]{1,0:T(8,128)S(1)} %get-tuple-element.1333), channel_id=1, source_target_pairs={{1,0},{2,1},{3,2},{4,3},{5,4},{6,5},{7,6},{8,7},{9,8},{10,9},{11,1... | collective-permute-start | bytes 786440 | tf_op jit(solution)/shard_map/while/body/eval_jaxpr/ppermute | solution.py:18
  338.4 9.2 %collective-permute-start.2 = (f32[128,512]{1,0:T(8,128)S(1)}, f32[128,512]{1,0:T(8,128)S(1)}, u32[]{:S(2)}, u32[]{:S(2)}) collective-permute-start(f32[128,512]{1,0:T(8,128)S(1)} %get-tuple-element.1333), channel_id=1, source_target_pairs={{1,0},{2,1},{3,2},{4,3},{5,4},{6,5},{7,6},{8,7},{9,8},{10,9},{11,1... | collective-permute-start | bytes 786440 | tf_op jit(solution)/shard_map/while/body/eval_jaxpr/ppermute | solution.py:18
  348.6 10.1 %collective-permute-start.2 = (f32[128,512]{1,0:T(8,128)S(1)}, f32[128,512]{1,0:T(8,128)S(1)}, u32[]{:S(2)}, u32[]{:S(2)}) collective-permute-start(f32[128,512]{1,0:T(8,128)S(1)} %get-tuple-element.1333), channel_id=1, source_target_pairs={{1,0},{2,1},{3,2},{4,3},{5,4},{6,5},{7,6},{8,7},{9,8},{10,9},{11,1... | collective-permute-start | bytes 786440 | tf_op jit(solution)/shard_map/while/body/eval_jaxpr/ppermute | solution.py:18
  359.7 11.7 %collective-permute-start.2 = (f32[128,512]{1,0:T(8,128)S(1)}, f32[128,512]{1,0:T(8,128)S(1)}, u32[]{:S(2)}, u32[]{:S(2)}) collective-permute-start(f32[128,512]{1,0:T(8,128)S(1)} %get-tuple-element.1333), channel_id=1, source_target_pairs={{1,0},{2,1},{3,2},{4,3},{5,4},{6,5},{7,6},{8,7},{9,8},{10,9},{11,1... | collective-permute-start | bytes 786440 | tf_op jit(solution)/shard_map/while/body/eval_jaxpr/ppermute | solution.py:18
  372.4 12.8 %collective-permute-start.2 = (f32[128,512]{1,0:T(8,128)S(1)}, f32[128,512]{1,0:T(8,128)S(1)}, u32[]{:S(2)}, u32[]{:S(2)}) collective-permute-start(f32[128,512]{1,0:T(8,128)S(1)} %get-tuple-element.1333), channel_id=1, source_target_pairs={{1,0},{2,1},{3,2},{4,3},{5,4},{6,5},{7,6},{8,7},{9,8},{10,9},{11,1... | collective-permute-start | bytes 786440 | tf_op jit(solution)/shard_map/while/body/eval_jaxpr/ppermute | solution.py:18
  (23 other events, 263.3 us)
where the time goes:
time: 567 us; the launch traced here: 564 us
  blocking collectives  175 us (31%)
  waiting for transfers between devices  139 us (25%)
  starting transfers between devices  136 us (24%)
  local copies, waits for them, and re-layouts  47.1 us (8%)
  matrix products  34.2 us (6%)
  other arithmetic  24 us (4%)
  loops' own time  6.87 us (1%)
    psum x1, blocking collectives, local(): grad_bias = lax.psum(jnp.sum(query_grad, axis=0), ('dp', 'ctx'))  175 us
    ppermute x45, waiting for transfers between devices, passed_along(): lax.ppermute(value, axis, [(source, source + steps) for source in range(f...  139 us
    ppermute x45, starting transfers between devices, passed_along(): lax.ppermute(value, axis, [(source, source + steps) for source in range(f...  136 us
    add x15, other arithmetic, return_partial(): returned + lax.dynamic_index_in_dim(partials, window_slots - 1 - step_ind...  14.8 us
  transfers between devices with their start and end apart: 45, of which 30 were waited for; matrix products, arithmetic and copies ran while one was open for 0% of the time, Pallas kernels for 0%

commit v1 on v0

--- a/solution.py
+++ b/solution.py
@@ -184,7 +184,8 @@
     summed_total = lax.fori_loop(1, window_slots, return_partial, partials[window_slots - 1])
     key_gradient = summed_total[:, : KEY_VALUE_HEADS * HEAD_SIZE].astype(jnp.bfloat16)
     value_gradient = summed_total[:, KEY_VALUE_HEADS * HEAD_SIZE :].astype(jnp.bfloat16)
-    grad_bias = lax.psum(jnp.sum(query_grad, axis=0), ("dp", "ctx"))
+    incoming_x = jnp.sum(query_grad, axis=0)
+    grad_bias = lax.psum(lax.psum(incoming_x, "ctx"), "dp")
     attended_out = attended.reshape(sharded_rows, QUERY_HEADS * HEAD_SIZE)
     return (
         attended_out[None],

time: 567 us -> 615 us (1.085)
  the two profiles are of different devices: /device:TPU:1 before, /device:TPU:385 now
where the time goes in v1:
time: 615 us; the launch traced here: 612 us
  blocking collectives  192 us (31%)
  starting transfers between devices  164 us (27%)
  waiting for transfers between devices  143 us (23%)
  local copies, waits for them, and re-layouts  47 us (8%)
  matrix products  34.2 us (6%)
  other arithmetic  23.9 us (4%)
  loops' own time  6.91 us (1%)
    psum x2, blocking collectives, local(): grad_bias = lax.psum(lax.psum(incoming_x, 'ctx'), 'dp')  192 us
    ppermute x45, starting transfers between devices, passed_along(): lax.ppermute(value, axis, [(source, source + steps) for source in range(f...  164 us
    ppermute x45, waiting for transfers between devices, passed_along(): lax.ppermute(value, axis, [(source, source + steps) for source in range(f...  143 us
    add x15, other arithmetic, return_partial(): returned + lax.dynamic_index_in_dim(partials, window_slots - 1 - step_ind...  14.8 us
  transfers between devices with their start and end apart: 45, of which 30 were waited for; matrix products, arithmetic and copies ran while one was open for 0% of the time, Pallas kernels for 0%

profile of v1, /device:TPU:385, one launch (start us, length us, event | category | flops | bytes accessed | tf_op | source)
XLA Modules:
  0.0 612.3 jit_solution(14547718030963852340)
XLA Ops:
  8.9 156.2 %while.72 = (s32[]{:T(128)}, bf16[16,128,512]{2,1,0:T(8,128)(2,1)}, s32[16,128]{1,0:T(8,128)S(1)}, bf16[128,512]{1,0:T(8,128)(2,1)S(1)}, s32[128]{0:T(128)S(1)}, /*index=5*/s32[]{:T(128)}, s32[]{:T(128)}, s32[]{:T(128)}) while((s32[]{:T(128)}, bf16[16,128,512]{2,1,0:T(8,128)(2,1)}, s32[16,128]{1,0:T(8,128)S(1)}, ...), condition=%wide.region_1.2_spmd, body=%wide.region_0.1_spmd.sunk | while | flops 5 | bytes 1052879 | solution.py:67
  96.0 5.9 collective-permute-done.1
  106.4 6.5 %collective-permute-done.1 = s32[128]{0:T(128)S(1)} collective-permute-done((s32[128]{0:T(128)S(1)}, s32[128]{0:T(128)S(1)}, u32[]{:S(2)}, u32[]{:S(2)}) %collective-permute-start.1) | collective-permute-done | bytes 544 | tf_op jit(solution)/shard_map/while/body/eval_jaxpr/ppermute | solution.py:18
  117.5 6.0 collective-permute-done.1
  169.3 23.1 %while.74 = (s32[]{:T(128)}, f32[2,7,128]{2,1,0:T(8,128)S(1)}, f32[2,7,128]{2,1,0:T(8,128)S(1)}, f32[2,7,128,128]{3,2,1,0:T(8,128)S(1)}, s32[4]{0:T(128)S(1)}, /...) while((s32[]{:T(128)}, f32[2,7,128]{2,1,0:T(8,128)S(1)}, ...), condition=%wide.region_5.6_spmd.clone.clone.clone, body=%wide.region_2.5_spmd.clone.clone.clone.sunk | while | flops 480120704 | bytes 16320205 | solution.py:125
  197.1 42.8 %while.75 = (s32[]{:T(128)}, f32[128,2,7,128]{0,3,2,1:T(8,128)S(1)}, f32[4,512,512]{2,1,0:T(8,128)}, bf16[4,512,512]{1,2,0:T(8,128)(2,1)}, s32[4]{0:T(128)S(1)},...) while((s32[]{:T(128)}, ...), condition=%wide.region_7.8_spmd.clone.clone.clone, body=%wide.region_6.7_spmd.clone.clone.clone.sunk | while | flops 1184918656 | bytes 30644960 | solution.py:170
  240.8 177.1 %while.73 = (s32[]{:T(128)}, f32[128,512]{1,0:T(8,128)S(1)}, f32[16,128,512]{2,1,0:T(8,128)}, s32[]{:T(128)}, s32[]{:T(128)}, /*index=5*/s32[]{:T(128)}, s32[]{:T(128)}) while((s32[]{:T(128)}, f32[128,512]{1,0:T(8,128)S(1)}, f32[16,128,512]{2,1,0:T(8,128)}, s32[]{:T(128)}, s32[]{:T(128)}, /*index=5*/s32[]{:T(128)}, s32[]{:T(128)}) %tuple.177), condition=%wide.region_9.10_spmd, body=%wide.region_8.9_spmd.sunk | while | flops 65542 | bytes 1835175 | solution.py:184
  248.9 6.7 %collective-permute-start.2 = (f32[128,512]{1,0:T(8,128)S(1)}, f32[128,512]{1,0:T(8,128)S(1)}, u32[]{:S(2)}, u32[]{:S(2)}) collective-permute-start(f32[128,512]{1,0:T(8,128)S(1)} %get-tuple-element.1333), channel_id=1, source_target_pairs={{1,0},{2,1},{3,2},{4,3},{5,4},{6,5},{7,6},{8,7},{9,8},{10,9},{11,1... | collective-permute-start | bytes 786440 | tf_op jit(solution)/shard_map/while/body/eval_jaxpr/ppermute | solution.py:18
  260.0 7.1 %collective-permute-start.2 = (f32[128,512]{1,0:T(8,128)S(1)}, f32[128,512]{1,0:T(8,128)S(1)}, u32[]{:S(2)}, u32[]{:S(2)}) collective-permute-start(f32[128,512]{1,0:T(8,128)S(1)} %get-tuple-element.1333), channel_id=1, source_target_pairs={{1,0},{2,1},{3,2},{4,3},{5,4},{6,5},{7,6},{8,7},{9,8},{10,9},{11,1... | collective-permute-start | bytes 786440 | tf_op jit(solution)/shard_map/while/body/eval_jaxpr/ppermute | solution.py:18
  271.4 7.1 %collective-permute-start.2 = (f32[128,512]{1,0:T(8,128)S(1)}, f32[128,512]{1,0:T(8,128)S(1)}, u32[]{:S(2)}, u32[]{:S(2)}) collective-permute-start(f32[128,512]{1,0:T(8,128)S(1)} %get-tuple-element.1333), channel_id=1, source_target_pairs={{1,0},{2,1},{3,2},{4,3},{5,4},{6,5},{7,6},{8,7},{9,8},{10,9},{11,1... | collective-permute-start | bytes 786440 | tf_op jit(solution)/shard_map/while/body/eval_jaxpr/ppermute | solution.py:18
  282.8 7.1 %collective-permute-start.2 = (f32[128,512]{1,0:T(8,128)S(1)}, f32[128,512]{1,0:T(8,128)S(1)}, u32[]{:S(2)}, u32[]{:S(2)}) collective-permute-start(f32[128,512]{1,0:T(8,128)S(1)} %get-tuple-element.1333), channel_id=1, source_target_pairs={{1,0},{2,1},{3,2},{4,3},{5,4},{6,5},{7,6},{8,7},{9,8},{10,9},{11,1... | collective-permute-start | bytes 786440 | tf_op jit(solution)/shard_map/while/body/eval_jaxpr/ppermute | solution.py:18
  294.8 7.1 %collective-permute-start.2 = (f32[128,512]{1,0:T(8,128)S(1)}, f32[128,512]{1,0:T(8,128)S(1)}, u32[]{:S(2)}, u32[]{:S(2)}) collective-permute-start(f32[128,512]{1,0:T(8,128)S(1)} %get-tuple-element.1333), channel_id=1, source_target_pairs={{1,0},{2,1},{3,2},{4,3},{5,4},{6,5},{7,6},{8,7},{9,8},{10,9},{11,1... | collective-permute-start | bytes 786440 | tf_op jit(solution)/shard_map/while/body/eval_jaxpr/ppermute | solution.py:18
  307.9 7.1 %collective-permute-start.2 = (f32[128,512]{1,0:T(8,128)S(1)}, f32[128,512]{1,0:T(8,128)S(1)}, u32[]{:S(2)}, u32[]{:S(2)}) collective-permute-start(f32[128,512]{1,0:T(8,128)S(1)} %get-tuple-element.1333), channel_id=1, source_target_pairs={{1,0},{2,1},{3,2},{4,3},{5,4},{6,5},{7,6},{8,7},{9,8},{10,9},{11,1... | collective-permute-start | bytes 786440 | tf_op jit(solution)/shard_map/while/body/eval_jaxpr/ppermute | solution.py:18
  315.1 6.1 collective-permute-done.2
  322.2 7.3 %collective-permute-start.2 = (f32[128,512]{1,0:T(8,128)S(1)}, f32[128,512]{1,0:T(8,128)S(1)}, u32[]{:S(2)}, u32[]{:S(2)}) collective-permute-start(f32[128,512]{1,0:T(8,128)S(1)} %get-tuple-element.1333), channel_id=1, source_target_pairs={{1,0},{2,1},{3,2},{4,3},{5,4},{6,5},{7,6},{8,7},{9,8},{10,9},{11,1... | collective-permute-start | bytes 786440 | tf_op jit(solution)/shard_map/while/body/eval_jaxpr/ppermute | solution.py:18
  335.8 7.4 %collective-permute-start.2 = (f32[128,512]{1,0:T(8,128)S(1)}, f32[128,512]{1,0:T(8,128)S(1)}, u32[]{:S(2)}, u32[]{:S(2)}) collective-permute-start(f32[128,512]{1,0:T(8,128)S(1)} %get-tuple-element.1333), channel_id=1, source_target_pairs={{1,0},{2,1},{3,2},{4,3},{5,4},{6,5},{7,6},{8,7},{9,8},{10,9},{11,1... | collective-permute-start | bytes 786440 | tf_op jit(solution)/shard_map/while/body/eval_jaxpr/ppermute | solution.py:18
  348.6 7.4 %collective-permute-start.2 = (f32[128,512]{1,0:T(8,128)S(1)}, f32[128,512]{1,0:T(8,128)S(1)}, u32[]{:S(2)}, u32[]{:S(2)}) collective-permute-start(f32[128,512]{1,0:T(8,128)S(1)} %get-tuple-element.1333), channel_id=1, source_target_pairs={{1,0},{2,1},{3,2},{4,3},{5,4},{6,5},{7,6},{8,7},{9,8},{10,9},{11,1... | collective-permute-start | bytes 786440 | tf_op jit(solution)/shard_map/while/body/eval_jaxpr/ppermute | solution.py:18
  360.3 7.6 %collective-permute-start.2 = (f32[128,512]{1,0:T(8,128)S(1)}, f32[128,512]{1,0:T(8,128)S(1)}, u32[]{:S(2)}, u32[]{:S(2)}) collective-permute-start(f32[128,512]{1,0:T(8,128)S(1)} %get-tuple-element.1333), channel_id=1, source_target_pairs={{1,0},{2,1},{3,2},{4,3},{5,4},{6,5},{7,6},{8,7},{9,8},{10,9},{11,1... | collective-permute-start | bytes 786440 | tf_op jit(solution)/shard_map/while/body/eval_jaxpr/ppermute | solution.py:18
  372.2 7.1 %collective-permute-start.2 = (f32[128,512]{1,0:T(8,128)S(1)}, f32[128,512]{1,0:T(8,128)S(1)}, u32[]{:S(2)}, u32[]{:S(2)}) collective-permute-start(f32[128,512]{1,0:T(8,128)S(1)} %get-tuple-element.1333), channel_id=1, source_target_pairs={{1,0},{2,1},{3,2},{4,3},{5,4},{6,5},{7,6},{8,7},{9,8},{10,9},{11,1... | collective-permute-start | bytes 786440 | tf_op jit(solution)/shard_map/while/body/eval_jaxpr/ppermute | solution.py:18
  383.6 7.1 %collective-permute-start.2 = (f32[128,512]{1,0:T(8,128)S(1)}, f32[128,512]{1,0:T(8,128)S(1)}, u32[]{:S(2)}, u32[]{:S(2)}) collective-permute-start(f32[128,512]{1,0:T(8,128)S(1)} %get-tuple-element.1333), channel_id=1, source_target_pairs={{1,0},{2,1},{3,2},{4,3},{5,4},{6,5},{7,6},{8,7},{9,8},{10,9},{11,1... | collective-permute-start | bytes 786440 | tf_op jit(solution)/shard_map/while/body/eval_jaxpr/ppermute | solution.py:18
  395.0 7.1 %collective-permute-start.2 = (f32[128,512]{1,0:T(8,128)S(1)}, f32[128,512]{1,0:T(8,128)S(1)}, u32[]{:S(2)}, u32[]{:S(2)}) collective-permute-start(f32[128,512]{1,0:T(8,128)S(1)} %get-tuple-element.1333), channel_id=1, source_target_pairs={{1,0},{2,1},{3,2},{4,3},{5,4},{6,5},{7,6},{8,7},{9,8},{10,9},{11,1... | collective-permute-start | bytes 786440 | tf_op jit(solution)/shard_map/while/body/eval_jaxpr/ppermute | solution.py:18
  406.5 7.1 %collective-permute-start.2 = (f32[128,512]{1,0:T(8,128)S(1)}, f32[128,512]{1,0:T(8,128)S(1)}, u32[]{:S(2)}, u32[]{:S(2)}) collective-permute-start(f32[128,512]{1,0:T(8,128)S(1)} %get-tuple-element.1333), channel_id=1, source_target_pairs={{1,0},{2,1},{3,2},{4,3},{5,4},{6,5},{7,6},{8,7},{9,8},{10,9},{11,1... | collective-permute-start | bytes 786440 | tf_op jit(solution)/shard_map/while/body/eval_jaxpr/ppermute | solution.py:18
  418.9 117.4 %psum.14 = f32[1792]{0:T(1024)S(1)} all-reduce(f32[1792]{0:T(1024)S(1)} %reduce_sum.25), channel_id=1, replica_groups=mesh['dp'=8,'ctx'=64] {'ctx'}, use_global_device_ids=true, to_apply=%region_11.12 | all-reduce | flops 1792 | bytes 14336 | tf_op jit(solution)/shard_map/psum | solution.py:188
  536.3 74.9 %psum.15 = f32[1792]{0:T(1024)} all-reduce(f32[1792]{0:T(1024)S(1)} %psum.14), channel_id=1, replica_groups=mesh['dp'=8,'ctx'=64] {'dp'}, use_global_device_ids=true, to_apply=%region_12.13 | all-reduce | flops 1792 | bytes 14336 | tf_op jit(solution)/shard_map/psum | solution.py:188
  (299 shorter events, 287.1 us)
Async XLA Ops:
  8.9 10.9 %collective-permute-start = (bf16[128,512]{1,0:T(8,128)(2,1)S(1)}, bf16[128,512]{1,0:T(8,128)(2,1)S(1)}, u32[]{:S(2)}, u32[]{:S(2)}) collective-permute-start(bf16[128,512]{1,0:T(8,128)(2,1)S(1)} %get-tuple-element.1222), channel_id=1, source_target_pairs={{0,1},{1,2},{2,3},{3,4},{4,5},{5,6},{6,7},{7,8},{8,9},{9,10},{10,1... | collective-permute-start | bytes 393224 | tf_op jit(solution)/shard_map/while/body/eval_jaxpr/ppermute | solution.py:18
  20.5 9.6 %collective-permute-start = (bf16[128,512]{1,0:T(8,128)(2,1)S(1)}, bf16[128,512]{1,0:T(8,128)(2,1)S(1)}, u32[]{:S(2)}, u32[]{:S(2)}) collective-permute-start(bf16[128,512]{1,0:T(8,128)(2,1)S(1)} %get-tuple-element.1222), channel_id=1, source_target_pairs={{0,1},{1,2},{2,3},{3,4},{4,5},{5,6},{6,7},{7,8},{8,9},{9,10},{10,1... | collective-permute-start | bytes 393224 | tf_op jit(solution)/shard_map/while/body/eval_jaxpr/ppermute | solution.py:18
  30.7 9.6 %collective-permute-start = (bf16[128,512]{1,0:T(8,128)(2,1)S(1)}, bf16[128,512]{1,0:T(8,128)(2,1)S(1)}, u32[]{:S(2)}, u32[]{:S(2)}) collective-permute-start(bf16[128,512]{1,0:T(8,128)(2,1)S(1)} %get-tuple-element.1222), channel_id=1, source_target_pairs={{0,1},{1,2},{2,3},{3,4},{4,5},{5,6},{6,7},{7,8},{8,9},{9,10},{10,1... | collective-permute-start | bytes 393224 | tf_op jit(solution)/shard_map/while/body/eval_jaxpr/ppermute | solution.py:18
  40.9 9.6 %collective-permute-start = (bf16[128,512]{1,0:T(8,128)(2,1)S(1)}, bf16[128,512]{1,0:T(8,128)(2,1)S(1)}, u32[]{:S(2)}, u32[]{:S(2)}) collective-permute-start(bf16[128,512]{1,0:T(8,128)(2,1)S(1)} %get-tuple-element.1222), channel_id=1, source_target_pairs={{0,1},{1,2},{2,3},{3,4},{4,5},{5,6},{6,7},{7,8},{8,9},{9,10},{10,1... | collective-permute-start | bytes 393224 | tf_op jit(solution)/shard_map/while/body/eval_jaxpr/ppermute | solution.py:18
  51.2 9.6 %collective-permute-start = (bf16[128,512]{1,0:T(8,128)(2,1)S(1)}, bf16[128,512]{1,0:T(8,128)(2,1)S(1)}, u32[]{:S(2)}, u32[]{:S(2)}) collective-permute-start(bf16[128,512]{1,0:T(8,128)(2,1)S(1)} %get-tuple-element.1222), channel_id=1, source_target_pairs={{0,1},{1,2},{2,3},{3,4},{4,5},{5,6},{6,7},{7,8},{8,9},{9,10},{10,1... | collective-permute-start | bytes 393224 | tf_op jit(solution)/shard_map/while/body/eval_jaxpr/ppermute | solution.py:18
  92.1 9.7 %collective-permute-start = (bf16[128,512]{1,0:T(8,128)(2,1)S(1)}, bf16[128,512]{1,0:T(8,128)(2,1)S(1)}, u32[]{:S(2)}, u32[]{:S(2)}) collective-permute-start(bf16[128,512]{1,0:T(8,128)(2,1)S(1)} %get-tuple-element.1222), channel_id=1, source_target_pairs={{0,1},{1,2},{2,3},{3,4},{4,5},{5,6},{6,7},{7,8},{8,9},{9,10},{10,1... | collective-permute-start | bytes 393224 | tf_op jit(solution)/shard_map/while/body/eval_jaxpr/ppermute | solution.py:18
  102.5 10.4 %collective-permute-start = (bf16[128,512]{1,0:T(8,128)(2,1)S(1)}, bf16[128,512]{1,0:T(8,128)(2,1)S(1)}, u32[]{:S(2)}, u32[]{:S(2)}) collective-permute-start(bf16[128,512]{1,0:T(8,128)(2,1)S(1)} %get-tuple-element.1222), channel_id=1, source_target_pairs={{0,1},{1,2},{2,3},{3,4},{4,5},{5,6},{6,7},{7,8},{8,9},{9,10},{10,1... | collective-permute-start | bytes 393224 | tf_op jit(solution)/shard_map/while/body/eval_jaxpr/ppermute | solution.py:18
  113.6 9.8 %collective-permute-start = (bf16[128,512]{1,0:T(8,128)(2,1)S(1)}, bf16[128,512]{1,0:T(8,128)(2,1)S(1)}, u32[]{:S(2)}, u32[]{:S(2)}) collective-permute-start(bf16[128,512]{1,0:T(8,128)(2,1)S(1)} %get-tuple-element.1222), channel_id=1, source_target_pairs={{0,1},{1,2},{2,3},{3,4},{4,5},{5,6},{6,7},{7,8},{8,9},{9,10},{10,1... | collective-permute-start | bytes 393224 | tf_op jit(solution)/shard_map/while/body/eval_jaxpr/ppermute | solution.py:18
  124.2 9.6 %collective-permute-start = (bf16[128,512]{1,0:T(8,128)(2,1)S(1)}, bf16[128,512]{1,0:T(8,128)(2,1)S(1)}, u32[]{:S(2)}, u32[]{:S(2)}) collective-permute-start(bf16[128,512]{1,0:T(8,128)(2,1)S(1)} %get-tuple-element.1222), channel_id=1, source_target_pairs={{0,1},{1,2},{2,3},{3,4},{4,5},{5,6},{6,7},{7,8},{8,9},{9,10},{10,1... | collective-permute-start | bytes 393224 | tf_op jit(solution)/shard_map/while/body/eval_jaxpr/ppermute | solution.py:18
  134.4 9.6 %collective-permute-start = (bf16[128,512]{1,0:T(8,128)(2,1)S(1)}, bf16[128,512]{1,0:T(8,128)(2,1)S(1)}, u32[]{:S(2)}, u32[]{:S(2)}) collective-permute-start(bf16[128,512]{1,0:T(8,128)(2,1)S(1)} %get-tuple-element.1222), channel_id=1, source_target_pairs={{0,1},{1,2},{2,3},{3,4},{4,5},{5,6},{6,7},{7,8},{8,9},{9,10},{10,1... | collective-permute-start | bytes 393224 | tf_op jit(solution)/shard_map/while/body/eval_jaxpr/ppermute | solution.py:18
  248.9 10.0 %collective-permute-start.2 = (f32[128,512]{1,0:T(8,128)S(1)}, f32[128,512]{1,0:T(8,128)S(1)}, u32[]{:S(2)}, u32[]{:S(2)}) collective-permute-start(f32[128,512]{1,0:T(8,128)S(1)} %get-tuple-element.1333), channel_id=1, source_target_pairs={{1,0},{2,1},{3,2},{4,3},{5,4},{6,5},{7,6},{8,7},{9,8},{10,9},{11,1... | collective-permute-start | bytes 786440 | tf_op jit(solution)/shard_map/while/body/eval_jaxpr/ppermute | solution.py:18
  260.0 10.4 %collective-permute-start.2 = (f32[128,512]{1,0:T(8,128)S(1)}, f32[128,512]{1,0:T(8,128)S(1)}, u32[]{:S(2)}, u32[]{:S(2)}) collective-permute-start(f32[128,512]{1,0:T(8,128)S(1)} %get-tuple-element.1333), channel_id=1, source_target_pairs={{1,0},{2,1},{3,2},{4,3},{5,4},{6,5},{7,6},{8,7},{9,8},{10,9},{11,1... | collective-permute-start | bytes 786440 | tf_op jit(solution)/shard_map/while/body/eval_jaxpr/ppermute | solution.py:18
  271.4 10.4 %collective-permute-start.2 = (f32[128,512]{1,0:T(8,128)S(1)}, f32[128,512]{1,0:T(8,128)S(1)}, u32[]{:S(2)}, u32[]{:S(2)}) collective-permute-start(f32[128,512]{1,0:T(8,128)S(1)} %get-tuple-element.1333), channel_id=1, source_target_pairs={{1,0},{2,1},{3,2},{4,3},{5,4},{6,5},{7,6},{8,7},{9,8},{10,9},{11,1... | collective-permute-start | bytes 786440 | tf_op jit(solution)/shard_map/while/body/eval_jaxpr/ppermute | solution.py:18
  282.8 11.0 %collective-permute-start.2 = (f32[128,512]{1,0:T(8,128)S(1)}, f32[128,512]{1,0:T(8,128)S(1)}, u32[]{:S(2)}, u32[]{:S(2)}) collective-permute-start(f32[128,512]{1,0:T(8,128)S(1)} %get-tuple-element.1333), channel_id=1, source_target_pairs={{1,0},{2,1},{3,2},{4,3},{5,4},{6,5},{7,6},{8,7},{9,8},{10,9},{11,1... | collective-permute-start | bytes 786440 | tf_op jit(solution)/shard_map/while/body/eval_jaxpr/ppermute | solution.py:18
  294.8 12.1 %collective-permute-start.2 = (f32[128,512]{1,0:T(8,128)S(1)}, f32[128,512]{1,0:T(8,128)S(1)}, u32[]{:S(2)}, u32[]{:S(2)}) collective-permute-start(f32[128,512]{1,0:T(8,128)S(1)} %get-tuple-element.1333), channel_id=1, source_target_pairs={{1,0},{2,1},{3,2},{4,3},{5,4},{6,5},{7,6},{8,7},{9,8},{10,9},{11,1... | collective-permute-start | bytes 786440 | tf_op jit(solution)/shard_map/while/body/eval_jaxpr/ppermute | solution.py:18
  307.9 13.2 %collective-permute-start.2 = (f32[128,512]{1,0:T(8,128)S(1)}, f32[128,512]{1,0:T(8,128)S(1)}, u32[]{:S(2)}, u32[]{:S(2)}) collective-permute-start(f32[128,512]{1,0:T(8,128)S(1)} %get-tuple-element.1333), channel_id=1, source_target_pairs={{1,0},{2,1},{3,2},{4,3},{5,4},{6,5},{7,6},{8,7},{9,8},{10,9},{11,1... | collective-permute-start | bytes 786440 | tf_op jit(solution)/shard_map/while/body/eval_jaxpr/ppermute | solution.py:18
  322.2 12.6 %collective-permute-start.2 = (f32[128,512]{1,0:T(8,128)S(1)}, f32[128,512]{1,0:T(8,128)S(1)}, u32[]{:S(2)}, u32[]{:S(2)}) collective-permute-start(f32[128,512]{1,0:T(8,128)S(1)} %get-tuple-element.1333), channel_id=1, source_target_pairs={{1,0},{2,1},{3,2},{4,3},{5,4},{6,5},{7,6},{8,7},{9,8},{10,9},{11,1... | collective-permute-start | bytes 786440 | tf_op jit(solution)/shard_map/while/body/eval_jaxpr/ppermute | solution.py:18
  335.8 11.8 %collective-permute-start.2 = (f32[128,512]{1,0:T(8,128)S(1)}, f32[128,512]{1,0:T(8,128)S(1)}, u32[]{:S(2)}, u32[]{:S(2)}) collective-permute-start(f32[128,512]{1,0:T(8,128)S(1)} %get-tuple-element.1333), channel_id=1, source_target_pairs={{1,0},{2,1},{3,2},{4,3},{5,4},{6,5},{7,6},{8,7},{9,8},{10,9},{11,1... | collective-permute-start | bytes 786440 | tf_op jit(solution)/shard_map/while/body/eval_jaxpr/ppermute | solution.py:18
  348.6 10.7 %collective-permute-start.2 = (f32[128,512]{1,0:T(8,128)S(1)}, f32[128,512]{1,0:T(8,128)S(1)}, u32[]{:S(2)}, u32[]{:S(2)}) collective-permute-start(f32[128,512]{1,0:T(8,128)S(1)} %get-tuple-element.1333), channel_id=1, source_target_pairs={{1,0},{2,1},{3,2},{4,3},{5,4},{6,5},{7,6},{8,7},{9,8},{10,9},{11,1... | collective-permute-start | bytes 786440 | tf_op jit(solution)/shard_map/while/body/eval_jaxpr/ppermute | solution.py:18
  360.3 10.9 %collective-permute-start.2 = (f32[128,512]{1,0:T(8,128)S(1)}, f32[128,512]{1,0:T(8,128)S(1)}, u32[]{:S(2)}, u32[]{:S(2)}) collective-permute-start(f32[128,512]{1,0:T(8,128)S(1)} %get-tuple-element.1333), channel_id=1, source_target_pairs={{1,0},{2,1},{3,2},{4,3},{5,4},{6,5},{7,6},{8,7},{9,8},{10,9},{11,1... | collective-permute-start | bytes 786440 | tf_op jit(solution)/shard_map/while/body/eval_jaxpr/ppermute | solution.py:18
  372.2 10.4 %collective-permute-start.2 = (f32[128,512]{1,0:T(8,128)S(1)}, f32[128,512]{1,0:T(8,128)S(1)}, u32[]{:S(2)}, u32[]{:S(2)}) collective-permute-start(f32[128,512]{1,0:T(8,128)S(1)} %get-tuple-element.1333), channel_id=1, source_target_pairs={{1,0},{2,1},{3,2},{4,3},{5,4},{6,5},{7,6},{8,7},{9,8},{10,9},{11,1... | collective-permute-start | bytes 786440 | tf_op jit(solution)/shard_map/while/body/eval_jaxpr/ppermute | solution.py:18
  383.6 10.4 %collective-permute-start.2 = (f32[128,512]{1,0:T(8,128)S(1)}, f32[128,512]{1,0:T(8,128)S(1)}, u32[]{:S(2)}, u32[]{:S(2)}) collective-permute-start(f32[128,512]{1,0:T(8,128)S(1)} %get-tuple-element.1333), channel_id=1, source_target_pairs={{1,0},{2,1},{3,2},{4,3},{5,4},{6,5},{7,6},{8,7},{9,8},{10,9},{11,1... | collective-permute-start | bytes 786440 | tf_op jit(solution)/shard_map/while/body/eval_jaxpr/ppermute | solution.py:18
  395.0 10.4 %collective-permute-start.2 = (f32[128,512]{1,0:T(8,128)S(1)}, f32[128,512]{1,0:T(8,128)S(1)}, u32[]{:S(2)}, u32[]{:S(2)}) collective-permute-start(f32[128,512]{1,0:T(8,128)S(1)} %get-tuple-element.1333), channel_id=1, source_target_pairs={{1,0},{2,1},{3,2},{4,3},{5,4},{6,5},{7,6},{8,7},{9,8},{10,9},{11,1... | collective-permute-start | bytes 786440 | tf_op jit(solution)/shard_map/while/body/eval_jaxpr/ppermute | solution.py:18
  406.5 10.4 %collective-permute-start.2 = (f32[128,512]{1,0:T(8,128)S(1)}, f32[128,512]{1,0:T(8,128)S(1)}, u32[]{:S(2)}, u32[]{:S(2)}) collective-permute-start(f32[128,512]{1,0:T(8,128)S(1)} %get-tuple-element.1333), channel_id=1, source_target_pairs={{1,0},{2,1},{3,2},{4,3},{5,4},{6,5},{7,6},{8,7},{9,8},{10,9},{11,1... | collective-permute-start | bytes 786440 | tf_op jit(solution)/shard_map/while/body/eval_jaxpr/ppermute | solution.py:18
  (23 other events, 331.6 us)
